TPU v7x, 256 devices: a whole 4x4x8 slice. The times are simulated.
256 devices in a mesh: sx: 8 (over z), sy: 32 (over y, x, core).
Axes of the slice: x: 4, y: 4, z: 8, core: 2. Of those that a mesh axis runs over, the one named last changes fastest.
Arguments:
- loads: float32 [12288, 4096], P('sx', 'sy'), may hold values from -6 to 6
- dual_op: bfloat16 [12288, 49152], P('sx', 'sy'), as said below
- dirichlet: bfloat16 [12288, 49152], P('sx', 'sy'), as said below
- corner_coupling: bfloat16 [128, 49152], P('sx', 'sy'), may hold values from -0.625 to 0.625
- corner_map: int32 [8, 512], P('sx', 'sy'), may hold values from 0 to 2047, as said below
- coarse_inverse: float32 [2048, 2048], P('sy'), as said below
Outputs:
- multipliers: float32 [12288, 4096], P('sx', 'sy')
- residual: float32 [12288, 4096], P('sx', 'sy')
Inputs may be any that keep to these rules, and one draw needn't show every extreme that they name: `corner_map`: every coarse unknown is named by exactly two entries over all subdomains. `dual_op`: each subdomain's block is symmetric positive definite. `dirichlet`: each subdomain's block is symmetric positive definite. `coarse_inverse`: symmetric positive definite.
All inputs are finite; a program needn't handle non-finite values.
Results may differ from a plain program's by a relative error of at most 0.014.
Values sent between devices are 32-bit elements; how exact they have to be, the bound alone decides.
No kernel may reach another device: no remote copies, remote signals or barrier semaphores. Data moves between devices by JAX's collectives and lax.ppermute only.
A program may use at most 64 MiB of HBM per device.

v0:
```python
import jax
import jax.numpy as jnp
from jax import lax
from jax.sharding import PartitionSpec as P

FACE = 320
EDGE = 64
ITERS = 4
HALF = 0.5
HIGH = lax.Precision.HIGHEST


def passed_along(value, axis, steps):
    count = lax.axis_size(axis)
    first, last = (max(0, -steps), min(count, count - steps))
    return lax.ppermute(value, axis, [(source, source + steps) for source in range(first, last)])


def padded(block, sides, width):
    for axis, dim in sides:
        count = lax.axis_size(axis)
        forward = [(i, i + 1) for i in range(count - 1)]
        backward = [(target, source) for source, target in forward]
        low = lax.ppermute(
            lax.slice_in_dim(block, block.shape[dim] - width, None, axis=dim), axis, forward
        )
        high = lax.ppermute(lax.slice_in_dim(block, 0, width, axis=dim), axis, backward)
        block = jnp.concatenate([low, block, high], axis=dim)
    return block


def split_blocks(field):
    widths = [FACE, FACE, FACE, FACE, EDGE, EDGE, EDGE, EDGE]
    pieces = []
    start = 0
    for width in widths:
        pieces.append(field[start : start + width])
        start = start + width
    return pieces


def assemble(field):
    pieces = split_blocks(field)
    upper_face = passed_along(pieces[1], "sx", 1)
    lower_face = passed_along(pieces[0], "sx", -1)
    left_face = passed_along(pieces[3], "sy", 1)
    right_face = passed_along(pieces[2], "sy", -1)
    stacked = jnp.concatenate([pieces[4], pieces[5], pieces[6], pieces[7]], axis=0)[None, None]
    bordered = padded(stacked, (("sx", 0), ("sy", 1)), 1)
    incoming = [
        upper_face,
        lower_face,
        left_face,
        right_face,
        bordered[0, 0, 3 * EDGE : 4 * EDGE],
        bordered[0, 2, 2 * EDGE : 3 * EDGE],
        bordered[2, 0, EDGE : 2 * EDGE],
        bordered[2, 2, 0:EDGE],
    ]
    return jnp.concatenate([mine + HALF * theirs for mine, theirs in zip(pieces, incoming)], axis=0)


def operate(direction, dual_op, corner_coupling, selector, coarse_inverse):
    spread = assemble(direction)
    rounded = spread.astype(jnp.bfloat16)
    local = jnp.dot(dual_op, rounded, preferred_element_type=jnp.float32)
    corner_part = jnp.dot(corner_coupling, rounded, preferred_element_type=jnp.float32)
    scattered = jnp.dot(selector.T, corner_part, precision=HIGH)
    coarse_sum = lax.psum(scattered, ("sx", "sy"))
    owned_rows = jnp.dot(coarse_inverse, coarse_sum, precision=HIGH)
    solution = lax.all_gather(owned_rows, "sy", axis=0, tiled=True)
    picked = jnp.dot(selector, solution, precision=HIGH)
    correction = jnp.dot(corner_coupling.astype(jnp.float32).T, picked, precision=HIGH)
    return assemble(local + correction)


def residual_norm(residual, smoothed):
    return lax.psum(jnp.sum(residual * smoothed, axis=0), ("sx", "sy"))


def body(loads, dual_op, dirichlet, corner_coupling, corner_map, coarse_inverse):
    corners = corner_map.shape[1]
    coarse_order = coarse_inverse.shape[1]
    selector = (
        corner_map[0][:, None] == lax.broadcasted_iota(jnp.int32, (corners, coarse_order), 1)
    ).astype(jnp.float32)

    def smooth(residual):
        return jnp.dot(dirichlet, residual.astype(jnp.bfloat16), preferred_element_type=jnp.float32)

    multipliers = jnp.zeros_like(loads)
    residual = loads
    smoothed = smooth(residual)
    direction = smoothed
    current = residual_norm(residual, smoothed)
    for step in range(ITERS):
        image = operate(direction, dual_op, corner_coupling, selector, coarse_inverse)
        alpha = current / lax.psum(jnp.sum(direction * image, axis=0), ("sx", "sy"))
        multipliers = multipliers + alpha * direction
        residual = residual - alpha * image
        if step + 1 < ITERS:
            smoothed = smooth(residual)
            following = residual_norm(residual, smoothed)
            direction = smoothed + following / current * direction
            current = following
    return (multipliers, residual)


def solution(mesh):
    in_specs = (
        P("sx", "sy"),
        P("sx", "sy"),
        P("sx", "sy"),
        P("sx", "sy"),
        P("sx", "sy"),
        P("sy", None),
    )
    out_specs = (P("sx", "sy"), P("sx", "sy"))
    return jax.shard_map(body, mesh=mesh, in_specs=in_specs, out_specs=out_specs, check_vma=False)
```

profile of v0, /device:TPU:1, one launch (start us, length us, event | category | flops | bytes accessed | tf_op | source)
XLA Modules:
  0.0 2106.7 jit_solution(1776008902199709787)
XLA Ops:
  12.6 5.0 collective-permute-start.4
  37.2 4.4 collective-permute-done.7
  43.7 265.5 %all-reduce.6.cloned.1.call-done = f32[2048,128]{1,0:T(8,128)} async-done(((f32[2048,128]{1,0:T(8,128)}), f32[2048,128]{1,0:T(8,128)}) %all-reduce.6.cloned.1.call-update) | async-done | bytes 1048592 | tf_op jit(solution)/shard_map/psum | solution.py:69
  315.6 45.0 %all-gather.5.cloned.1.call-done = f32[2048,128]{1,0:T(8,128)} async-done(((f32[64,128]{1,0:T(8,128)}), f32[2048,128]{1,0:T(8,128)}) %all-gather.5.cloned.1.call-update) | async-done | bytes 1048592 | tf_op jit(solution)/shard_map/all_gather | solution.py:71
  373.4 4.5 collective-permute-start.14
  385.7 4.4 collective-permute-done.11
  391.3 82.7 %all-reduce = (f32[128]{0:T(128)S(1)}, f32[128]{0:T(128)S(1)}) all-reduce(f32[128]{0:T(128)S(1)} %get-tuple-element.3, f32[128]{0:T(128)S(1)} %get-tuple-element.2), channel_id=1, replica_groups=mesh['sx'=8,'sy'=32] {'sx','sy'}, use_global_device_ids=true, to_apply=%region_1.0 | all-reduce | flops 256 | bytes 2048 | tf_op jit(solution)/shard_map/psum | solution.py:78
  475.3 4.6 multiply_reduce_fusion.5
  479.9 74.7 %psum.87 = f32[128]{0:T(128)S(1)} all-reduce(f32[128]{0:T(128)S(1)} %get-tuple-element.40), channel_id=1, replica_groups=mesh['sx'=8,'sy'=32] {'sx','sy'}, use_global_device_ids=true, to_apply=%region_6.0 | all-reduce | flops 128 | bytes 1024 | tf_op jit(solution)/shard_map/psum | solution.py:78
  578.8 4.4 collective-permute-done.23
  585.6 263.1 %all-reduce.8.cloned.1.call-done = f32[2048,128]{1,0:T(8,128)} async-done(((f32[2048,128]{1,0:T(8,128)}), f32[2048,128]{1,0:T(8,128)}) %all-reduce.8.cloned.1.call-update) | async-done | bytes 1048592 | tf_op jit(solution)/shard_map/psum | solution.py:69
  851.3 4.6 fusion.123
  856.0 44.0 %all-gather.7.cloned.1.call-done = f32[2048,128]{1,0:T(8,128)} async-done(((f32[64,128]{1,0:T(8,128)}), f32[2048,128]{1,0:T(8,128)}) %all-gather.7.cloned.1.call-update) | async-done | bytes 1048592 | tf_op jit(solution)/shard_map/all_gather | solution.py:71
  913.8 4.5 collective-permute-start.30
  931.7 82.7 %psum.89 = f32[128]{0:T(128)S(1)} all-reduce(f32[128]{0:T(128)S(1)} %multiply_reduce_fusion.4), channel_id=1, replica_groups=mesh['sx'=8,'sy'=32] {'sx','sy'}, use_global_device_ids=true, to_apply=%region_9.0 | all-reduce | flops 128 | bytes 1024 | tf_op jit(solution)/shard_map/psum | solution.py:98
  1016.5 4.6 multiply_reduce_fusion.3
  1021.2 74.7 %psum.90 = f32[128]{0:T(128)S(1)} all-reduce(f32[128]{0:T(128)S(1)} %get-tuple-element.42), channel_id=1, replica_groups=mesh['sx'=8,'sy'=32] {'sx','sy'}, use_global_device_ids=true, to_apply=%region_11.0 | all-reduce | flops 128 | bytes 1024 | tf_op jit(solution)/shard_map/psum | solution.py:78
  1120.1 4.4 collective-permute-done.39
  1126.6 263.3 %all-reduce.10.cloned.1.call-done = f32[2048,128]{1,0:T(8,128)} async-done(((f32[2048,128]{1,0:T(8,128)}), f32[2048,128]{1,0:T(8,128)}) %all-reduce.10.cloned.1.call-update) | async-done | bytes 1048592 | tf_op jit(solution)/shard_map/psum | solution.py:69
  1392.6 4.6 fusion.124
  1397.2 43.7 %all-gather.9.cloned.1.call-done = f32[2048,128]{1,0:T(8,128)} async-done(((f32[64,128]{1,0:T(8,128)}), f32[2048,128]{1,0:T(8,128)}) %all-gather.9.cloned.1.call-update) | async-done | bytes 1048592 | tf_op jit(solution)/shard_map/all_gather | solution.py:71
  1454.8 4.5 collective-permute-start.46
  1472.7 82.7 %psum.92 = f32[128]{0:T(128)S(1)} all-reduce(f32[128]{0:T(128)S(1)} %multiply_reduce_fusion.2), channel_id=1, replica_groups=mesh['sx'=8,'sy'=32] {'sx','sy'}, use_global_device_ids=true, to_apply=%region_14.0 | all-reduce | flops 128 | bytes 1024 | tf_op jit(solution)/shard_map/psum | solution.py:98
  1557.8 4.6 multiply_reduce_fusion.1
  1562.4 74.8 %psum.93 = f32[128]{0:T(128)S(1)} all-reduce(f32[128]{0:T(128)S(1)} %get-tuple-element.44), channel_id=1, replica_groups=mesh['sx'=8,'sy'=32] {'sx','sy'}, use_global_device_ids=true, to_apply=%region_16.0 | all-reduce | flops 128 | bytes 1024 | tf_op jit(solution)/shard_map/psum | solution.py:78
  1661.4 4.4 collective-permute-done.55
  1667.9 263.3 %all-reduce.12.cloned.1.call-done = f32[2048,128]{1,0:T(8,128)} async-done(((f32[2048,128]{1,0:T(8,128)}), f32[2048,128]{1,0:T(8,128)}) %all-reduce.12.cloned.1.call-update) | async-done | bytes 1048592 | tf_op jit(solution)/shard_map/psum | solution.py:69
  1933.9 4.6 fusion.125
  1938.5 43.8 %all-gather.11.cloned.1.call-done = f32[2048,128]{1,0:T(8,128)} async-done(((f32[64,128]{1,0:T(8,128)}), f32[2048,128]{1,0:T(8,128)}) %all-gather.11.cloned.1.call-update) | async-done | bytes 1048592 | tf_op jit(solution)/shard_map/all_gather | solution.py:71
  1996.2 4.5 collective-permute-start.62
  2008.5 4.4 collective-permute-done.59
  2014.1 82.7 %psum.95 = f32[128]{0:T(128)S(1)} all-reduce(f32[128]{0:T(128)S(1)} %multiply_reduce_fusion), channel_id=1, replica_groups=mesh['sx'=8,'sy'=32] {'sx','sy'}, use_global_device_ids=true, to_apply=%region_19.0 | all-reduce | flops 128 | bytes 1024 | tf_op jit(solution)/shard_map/psum | solution.py:98
  (285 shorter events, 227.6 us)
Async XLA Ops:
  7.2 302.0 %all-reduce.6.cloned.1.call-start = ((), (), s32[]{:S(2)}) async-start(), calls=%async_computation | async-start | bytes 2097152 | tf_op jit(solution)/shard_map/psum | solution.py:69
  11.3 15.6 collective-permute-start.5
  12.6 16.2 collective-permute-start.4
  17.6 14.8 collective-permute-start
  21.2 13.3 collective-permute-start.1
  43.7 316.9 %all-gather.5.cloned.1.call-start = ((), (), s32[]{:S(2)}) async-start(), calls=%async_computation.1 | async-start | bytes 1081344 | tf_op jit(solution)/shard_map/all_gather | solution.py:71
  311.8 536.8 %all-reduce.8.cloned.1.call-start = ((), (), s32[]{:S(2)}) async-start(), calls=%async_computation.2 | async-start | bytes 2097152 | tf_op jit(solution)/shard_map/psum | solution.py:69
  371.5 13.9 collective-permute-start.9
  373.4 16.7 collective-permute-start.14
  555.8 12.7 collective-permute-start.21
  557.1 13.3 collective-permute-start.20
  561.2 13.0 collective-permute-start.16
  563.1 13.0 collective-permute-start.17
  585.3 314.6 %all-gather.7.cloned.1.call-start = ((), (), s32[]{:S(2)}) async-start(), calls=%async_computation.3 | async-start | bytes 1081344 | tf_op jit(solution)/shard_map/all_gather | solution.py:71
  851.3 538.6 %all-reduce.10.cloned.1.call-start = ((), (), s32[]{:S(2)}) async-start(), calls=%async_computation.4 | async-start | bytes 2097152 | tf_op jit(solution)/shard_map/psum | solution.py:69
  911.9 13.9 collective-permute-start.25
  913.8 16.7 collective-permute-start.30
  1097.1 12.7 collective-permute-start.37
  1098.4 13.3 collective-permute-start.36
  1102.4 13.0 collective-permute-start.32
  1104.4 13.0 collective-permute-start.33
  1126.6 314.4 %all-gather.9.cloned.1.call-start = ((), (), s32[]{:S(2)}) async-start(), calls=%async_computation.5 | async-start | bytes 1081344 | tf_op jit(solution)/shard_map/all_gather | solution.py:71
  1392.6 538.7 %all-reduce.12.cloned.1.call-start = ((), (), s32[]{:S(2)}) async-start(), calls=%async_computation.6 | async-start | bytes 2097152 | tf_op jit(solution)/shard_map/psum | solution.py:69
  1452.9 14.1 collective-permute-start.41
  1454.8 16.7 collective-permute-start.46
  1638.5 12.5 collective-permute-start.53
  1639.8 13.2 collective-permute-start.52
  1643.8 12.8 collective-permute-start.48
  1645.8 12.9 collective-permute-start.49
  1667.9 314.4 %all-gather.11.cloned.1.call-start = ((), (), s32[]{:S(2)}) async-start(), calls=%async_computation.7 | async-start | bytes 1081344 | tf_op jit(solution)/shard_map/all_gather | solution.py:71
  1994.3 13.9 collective-permute-start.57
  1996.2 16.7 collective-permute-start.62
  (52 other events, 842.2 us)
Sparse Core Ops, SparseCore 0:
  43.8 265.3 all-reduce.5
  312.3 48.2 all-gather.4
  585.4 263.1 all-reduce.7
  851.6 48.2 all-gather.6
  1126.7 263.1 all-reduce.9
  1392.7 48.2 all-gather.8
  1668.0 263.2 all-reduce.11
  1934.0 48.2 all-gather.10
where the time goes:
time: 2110 us
  waiting for transfers between devices  1280 us (61%)
  blocking collectives  555 us (26%)
  starting transfers between devices  171 us (8%)
  matrix products  66.4 us (3%)
    psum x4, waiting for transfers between devices, operate(): coarse_sum = lax.psum(scattered, ('sx', 'sy'))  1060 us
    psum x4, blocking collectives, residual_norm(): return lax.psum(jnp.sum(residual * smoothed, axis=0), ('sx', 'sy'))  307 us
    psum x3, blocking collectives, body(): alpha = current / lax.psum(jnp.sum(direction * image, axis=0), ('sx', 'sy'))  248 us
    all_gather x4, waiting for transfers between devices, operate(): solution = lax.all_gather(owned_rows, 'sy', axis=0, tiled=True)  176 us
    ppermute x32, starting transfers between devices, passed_along(): lax.ppermute(value, axis, [(source, source + steps) for source in range(f...  79 us
    ppermute x16, starting transfers between devices, padded(): lax.ppermute(lax.slice_in_dim(block, block.shape[dim] - width, None, axis...  65.3 us
  transfers between devices with their start and end apart: 72, of which 28 were waited for; matrix products, arithmetic and copies ran while one was open for 1% of the time, Pallas kernels for 0%

commit v1 on v0

--- a/solution.py
+++ b/solution.py
@@ -68,7 +68,9 @@
     scattered = jnp.dot(selector.T, corner_part, precision=HIGH)
     coarse_sum = lax.psum(scattered, ("sx", "sy"))
     owned_rows = jnp.dot(coarse_inverse, coarse_sum, precision=HIGH)
-    solution = lax.all_gather(owned_rows, "sy", axis=0, tiled=True)
+    solution = jnp.concatenate(
+        lax.all_to_all(jnp.stack([owned_rows] * lax.axis_size("sy")), "sy", 0, 0), axis=0
+    )
     picked = jnp.dot(selector, solution, precision=HIGH)
     correction = jnp.dot(corner_coupling.astype(jnp.float32).T, picked, precision=HIGH)
     return assemble(local + correction)

time: 2110 us -> 2020 us (0.957)
  waiting for transfers between devices: 1280 us -> 1150 us
  starting transfers between devices: 171 us -> 203 us
    all_gather x4 -> x0, waiting for transfers between devices: 176 us -> none  [operate(): solution = lax.all_gather(owned_rows, 'sy', axis=0, tiled=True)]
    all_to_all x0 -> x4, waiting for transfers between devices: none -> 40.1 us  [operate(): lax.all_to_all(jnp.stack([owned_rows] * lax.axis_size('sy')), 'sy', 0, 0)]
    all_to_all x0 -> x4, starting transfers between devices: none -> 34.1 us  [operate(): lax.all_to_all(jnp.stack([owned_rows] * lax.axis_size('sy')), 'sy', 0, 0)]
where the time goes in v1:
time: 2020 us; the launch traced here: 2010 us
  waiting for transfers between devices  1150 us (57%)
  blocking collectives  553 us (27%)
  starting transfers between devices  203 us (10%)
  matrix products  65 us (3%)
    psum x4, waiting for transfers between devices, operate(): coarse_sum = lax.psum(scattered, ('sx', 'sy'))  1060 us
    psum x4, blocking collectives, residual_norm(): return lax.psum(jnp.sum(residual * smoothed, axis=0), ('sx', 'sy'))  307 us
    psum x3, blocking collectives, body(): alpha = current / lax.psum(jnp.sum(direction * image, axis=0), ('sx', 'sy'))  246 us
    ppermute x32, starting transfers between devices, passed_along(): lax.ppermute(value, axis, [(source, source + steps) for source in range(f...  70.6 us
    ppermute x16, starting transfers between devices, padded(): lax.ppermute(lax.slice_in_dim(block, block.shape[dim] - width, None, axis...  62.7 us
  transfers between devices with their start and end apart: 72, of which 28 were waited for; matrix products, arithmetic and copies ran while one was open for 1% of the time, Pallas kernels for 0%

profile of v1, /device:TPU:1, one launch (start us, length us, event | category | flops | bytes accessed | tf_op | source)
XLA Modules:
  0.0 2007.0 jit_solution(16078455720477667792)
XLA Ops:
  12.6 5.0 collective-permute-start.4
  37.2 4.4 collective-permute-done.7
  43.7 265.7 %all-reduce.6.cloned.1.call-done = f32[2048,128]{1,0:T(8,128)} async-done(((f32[2048,128]{1,0:T(8,128)}), f32[2048,128]{1,0:T(8,128)}) %all-reduce.6.cloned.1.call-update) | async-done | bytes 1048592 | tf_op jit(solution)/shard_map/psum | solution.py:69
  312.5 8.5 all-to-all-start
  321.0 4.6 fusion.122
  325.6 12.4 all-to-all-done
  366.3 81.9 %all-reduce = (f32[128]{0:T(128)S(1)}, f32[128]{0:T(128)S(1)}) all-reduce(f32[128]{0:T(128)S(1)} %get-tuple-element.3, f32[128]{0:T(128)S(1)} %get-tuple-element.2), channel_id=1, replica_groups=mesh['sx'=8,'sy'=32] {'sx','sy'}, use_global_device_ids=true, to_apply=%region_1.0 | all-reduce | flops 256 | bytes 2048 | tf_op jit(solution)/shard_map/psum | solution.py:80
  449.4 4.6 multiply_reduce_fusion.5
  454.0 75.1 %psum.87 = f32[128]{0:T(128)S(1)} all-reduce(f32[128]{0:T(128)S(1)} %get-tuple-element.40), channel_id=1, replica_groups=mesh['sx'=8,'sy'=32] {'sx','sy'}, use_global_device_ids=true, to_apply=%region_6.0 | all-reduce | flops 128 | bytes 1024 | tf_op jit(solution)/shard_map/psum | solution.py:80
  553.2 4.4 collective-permute-done.23
  560.5 263.4 %all-reduce.8.cloned.1.call-done = f32[2048,128]{1,0:T(8,128)} async-done(((f32[2048,128]{1,0:T(8,128)}), f32[2048,128]{1,0:T(8,128)}) %all-reduce.8.cloned.1.call-update) | async-done | bytes 1048592 | tf_op jit(solution)/shard_map/psum | solution.py:69
  827.0 8.5 all-to-all-start.1
  835.6 4.7 fusion.123
  840.3 12.4 all-to-all-done.1
  876.5 4.4 collective-permute-done.27
  882.1 81.9 %psum.89 = f32[128]{0:T(128)S(1)} all-reduce(f32[128]{0:T(128)S(1)} %multiply_reduce_fusion.4), channel_id=1, replica_groups=mesh['sx'=8,'sy'=32] {'sx','sy'}, use_global_device_ids=true, to_apply=%region_9.0 | all-reduce | flops 128 | bytes 1024 | tf_op jit(solution)/shard_map/psum | solution.py:100
  966.0 4.6 multiply_reduce_fusion.3
  970.7 75.2 %psum.90 = f32[128]{0:T(128)S(1)} all-reduce(f32[128]{0:T(128)S(1)} %get-tuple-element.42), channel_id=1, replica_groups=mesh['sx'=8,'sy'=32] {'sx','sy'}, use_global_device_ids=true, to_apply=%region_11.0 | all-reduce | flops 128 | bytes 1024 | tf_op jit(solution)/shard_map/psum | solution.py:80
  1069.9 4.4 collective-permute-done.39
  1077.2 263.3 %all-reduce.10.cloned.1.call-done = f32[2048,128]{1,0:T(8,128)} async-done(((f32[2048,128]{1,0:T(8,128)}), f32[2048,128]{1,0:T(8,128)}) %all-reduce.10.cloned.1.call-update) | async-done | bytes 1048592 | tf_op jit(solution)/shard_map/psum | solution.py:69
  1343.6 8.5 all-to-all-start.2
  1352.1 9.4 all-reduce.12.cloned.1.call-start
  1361.6 4.7 fusion.124
  1398.7 81.9 %psum.92 = f32[128]{0:T(128)S(1)} all-reduce(f32[128]{0:T(128)S(1)} %multiply_reduce_fusion.2), channel_id=1, replica_groups=mesh['sx'=8,'sy'=32] {'sx','sy'}, use_global_device_ids=true, to_apply=%region_14.0 | all-reduce | flops 128 | bytes 1024 | tf_op jit(solution)/shard_map/psum | solution.py:100
  1482.9 4.6 multiply_reduce_fusion.1
  1487.5 75.2 %psum.93 = f32[128]{0:T(128)S(1)} all-reduce(f32[128]{0:T(128)S(1)} %get-tuple-element.44), channel_id=1, replica_groups=mesh['sx'=8,'sy'=32] {'sx','sy'}, use_global_device_ids=true, to_apply=%region_16.0 | all-reduce | flops 128 | bytes 1024 | tf_op jit(solution)/shard_map/psum | solution.py:80
  1586.7 4.4 collective-permute-done.55
  1594.0 263.3 %all-reduce.12.cloned.1.call-done = f32[2048,128]{1,0:T(8,128)} async-done(((f32[2048,128]{1,0:T(8,128)}), f32[2048,128]{1,0:T(8,128)}) %all-reduce.12.cloned.1.call-update) | async-done | bytes 1048592 | tf_op jit(solution)/shard_map/psum | solution.py:69
  1860.4 8.5 all-to-all-start.3
  1869.0 4.7 fusion.125
  1873.7 12.4 all-to-all-done.3
  1915.6 81.9 %psum.95 = f32[128]{0:T(128)S(1)} all-reduce(f32[128]{0:T(128)S(1)} %multiply_reduce_fusion), channel_id=1, replica_groups=mesh['sx'=8,'sy'=32] {'sx','sy'}, use_global_device_ids=true, to_apply=%region_19.0 | all-reduce | flops 128 | bytes 1024 | tf_op jit(solution)/shard_map/psum | solution.py:100
  (291 shorter events, 242.8 us)
Async XLA Ops:
  7.2 302.1 %all-reduce.6.cloned.1.call-start = ((), (), s32[]{:S(2)}) async-start(), calls=%async_computation.4 | async-start | bytes 2097152 | tf_op jit(solution)/shard_map/psum | solution.py:69
  11.3 15.6 collective-permute-start.5
  12.6 16.2 collective-permute-start.4
  17.6 14.8 collective-permute-start
  21.2 13.3 collective-permute-start.1
  312.5 25.5 %all-to-all-start = ((f32[32,64,128]{2,1,0:T(8,128)}), f32[32,64,128]{2,1,0:T(8,128)S(1)}, u32[]{:S(2)}, u32[]{:S(2)}) async-start(f32[32,64,128]{2,1,0:T(8,128)} %stack.8), calls=%async_computation | async-start | bytes 2097152 | tf_op jit(solution)/shard_map/all_to_all | solution.py:72
  321.0 502.9 %all-reduce.8.cloned.1.call-start = ((), (), s32[]{:S(2)}) async-start(), calls=%async_computation.5 | async-start | bytes 2097152 | tf_op jit(solution)/shard_map/psum | solution.py:69
  346.9 13.4 collective-permute-start.9
  349.0 16.0 collective-permute-start.14
  530.4 12.5 collective-permute-start.21
  531.7 13.1 collective-permute-start.20
  535.7 12.8 collective-permute-start.16
  537.7 13.1 collective-permute-start.17
  827.0 25.6 %all-to-all-start.1 = ((f32[32,64,128]{2,1,0:T(8,128)}), f32[32,64,128]{2,1,0:T(8,128)}, u32[]{:S(2)}, u32[]{:S(2)}) async-start(f32[32,64,128]{2,1,0:T(8,128)} %stack.9), calls=%async_computation.1 | async-start | bytes 2097152 | tf_op jit(solution)/shard_map/all_to_all | solution.py:72
  835.5 505.0 %all-reduce.10.cloned.1.call-start = ((), (), s32[]{:S(2)}) async-start(), calls=%async_computation.6 | async-start | bytes 2097152 | tf_op jit(solution)/shard_map/psum | solution.py:69
  862.7 13.4 collective-permute-start.25
  864.8 16.0 collective-permute-start.30
  1047.2 12.4 collective-permute-start.37
  1048.5 13.0 collective-permute-start.36
  1052.5 12.7 collective-permute-start.32
  1054.4 12.7 collective-permute-start.33
  1343.6 25.6 %all-to-all-start.2 = ((f32[32,64,128]{2,1,0:T(8,128)}), f32[32,64,128]{2,1,0:T(8,128)}, u32[]{:S(2)}, u32[]{:S(2)}) async-start(f32[32,64,128]{2,1,0:T(8,128)} %stack.10), calls=%async_computation.2 | async-start | bytes 2097152 | tf_op jit(solution)/shard_map/all_to_all | solution.py:72
  1352.1 505.2 %all-reduce.12.cloned.1.call-start = ((), (), s32[]{:S(2)}) async-start(), calls=%async_computation.7 | async-start | bytes 2097152 | tf_op jit(solution)/shard_map/psum | solution.py:69
  1379.3 13.4 collective-permute-start.41
  1381.5 16.0 collective-permute-start.46
  1564.0 12.4 collective-permute-start.53
  1565.3 13.0 collective-permute-start.52
  1569.4 12.7 collective-permute-start.48
  1571.3 12.7 collective-permute-start.49
  1860.4 25.6 %all-to-all-start.3 = ((f32[32,64,128]{2,1,0:T(8,128)}), f32[32,64,128]{2,1,0:T(8,128)}, u32[]{:S(2)}, u32[]{:S(2)}) async-start(f32[32,64,128]{2,1,0:T(8,128)} %stack.11), calls=%async_computation.3 | async-start | bytes 2097152 | tf_op jit(solution)/shard_map/all_to_all | solution.py:72
  1896.3 13.4 collective-permute-start.57
  1898.4 16.0 collective-permute-start.62
  (55 other events, 800.5 us)
Sparse Core Ops, SparseCore 0:
  43.8 265.4 all-reduce.5
  560.6 263.2 all-reduce.7
  1077.3 263.1 all-reduce.9
  1594.1 263.1 all-reduce.11
